TPU v7x, 32 devices: a whole 2x2x4 slice. The times are simulated.
32 devices in a mesh: groups: 2 (over x), ctx: 4 (over y, core), heads: 4 (over z).
Axes of the slice: x: 2, y: 2, z: 4, core: 2. Of those that a mesh axis runs over, the one named last changes fastest.
Arguments:
- tokens: bfloat16 [4096, 2048], P(('groups', 'ctx', 'heads')), parts along dimension 0, may hold values from -60 to 60
- state_in: float32 [4, 256, 128], P('heads', 'groups'), parts along dimension 1, may hold values from -256 to 256
- past_kv: bfloat16 [2, 1024, 512], P(None, 'groups', 'heads'), parts along dimension 1, may hold values from -6 to 6
- w_qkv: bfloat16 [2048, 3, 512], P(None, None, 'heads'), may hold values from -0.125 to 0.125
- w_out: bfloat16 [512, 2048], P('heads'), may hold values from -0.25 to 0.25
- w_gate: bfloat16 [16, 2048, 768], P(('ctx', 'heads')), may hold values from -0.125 to 0.125
- w_up: bfloat16 [16, 2048, 768], P(('ctx', 'heads')), may hold values from -0.125 to 0.125
- w_down: bfloat16 [16, 768, 2048], P(('ctx', 'heads')), may hold values from -0.21875 to 0.21875
- expert_ids: int32 [4096, 8], P(('groups', 'ctx', 'heads')), parts along dimension 0, may hold values from 0 to 15, all different within a row; in each aligned block of 128 rows (0 to 127, 128 to 255, ...) at most 128 rows name the same one
- gate_weights: float32 [4096, 8], P(('groups', 'ctx', 'heads')), parts along dimension 0, may hold values from 0.1 to 1
Outputs:
- mixed: bfloat16 [4096, 2048], P(('groups', 'ctx', 'heads')), parts along dimension 0
There are 2 independent parts, one for each index of `groups`. A program takes and returns all parts, laid end to end along the dimension named above; an argument that names none is the same for every part. Nothing has to cross between parts.
Inputs may be any that keep to these rules, and one draw needn't show every extreme that they name: `expert_ids`: each row names 8 different experts; in each aligned block of 128 rows (the rows of one device) no expert is named by more than 128 rows, a bound that some block reaches.
All inputs are finite; a program needn't handle non-finite values.
Results may differ from a plain program's by a relative error of at most 0.017.
Values may be sent and summed in bfloat16 or wider, within the bound.
A program may use at most 128 MiB of HBM per device.

v0:
```python
import math
import jax
import jax.numpy as jnp
from jax import lax
from jax.sharding import PartitionSpec as P

HDIM = 128
WINDOW = 512


def entering(x, axis, join, neutral):
    place = lax.axis_index(axis)
    gathered = lax.all_gather(x.astype(jnp.bfloat16), axis)
    state = jnp.zeros_like(x) + jnp.asarray(neutral, x.dtype)

    def one(lap, state):
        return join(state, lax.dynamic_index_in_dim(gathered, lap, 0, False).astype(x.dtype))

    return lax.fori_loop(0, place, one, state)


def from_behind(block, axis, distance):
    devices = range(lax.axis_size(axis))
    route = [(i - distance, i) for i in devices if i - distance in devices]
    return lax.ppermute(block, axis, route)


def normalize(value):
    return value * lax.rsqrt(jnp.mean(value * value, axis=-1, keepdims=True) + 1e-06)


def dense_experts(
    hidden_float, normed, w_gate, w_up, w_down, expert_ids, gate_weights, expert_count
):
    axes = ("ctx", "heads")
    exp_local = w_gate.shape[0]
    chosen = expert_ids[:, :, None] == jnp.arange(expert_count, dtype=jnp.int32)
    table = jnp.sum(jnp.where(chosen, gate_weights[:, :, None], 0.0), axis=1)
    weights = lax.all_gather(table, axes, axis=0, tiled=True)
    first = lax.axis_index(axes) * exp_local
    rows = lax.all_gather(normed, axes, axis=0, tiled=True)
    total = None
    for e in range(exp_local):
        gate_act = jnp.dot(rows, w_gate[e], preferred_element_type=jnp.float32)
        up_act = jnp.dot(rows, w_up[e], preferred_element_type=jnp.float32)
        hid = (jax.nn.silu(gate_act) * up_act).astype(jnp.bfloat16)
        out_rows = jnp.dot(hid, w_down[e], preferred_element_type=jnp.float32)
        weight = lax.dynamic_slice_in_dim(weights, first + e, 1, 1)
        part = weight * out_rows
        total = part if total is None else total + part
    routed = lax.psum_scatter(total.astype(jnp.bfloat16), axes, scatter_dimension=0, tiled=True)
    return (hidden_float + routed.astype(jnp.float32)).astype(jnp.bfloat16)


def on_device(
    tokens, state_in, past_kv, w_qkv, w_out, w_gate, w_up, w_down, expert_ids, gate_weights
):
    row_count, model_width = tokens.shape
    inner_width = w_qkv.shape[2]
    local_heads = inner_width // HDIM
    w_flat = w_qkv.reshape(model_width, 3 * inner_width)
    projected = jnp.dot(
        lax.all_gather(tokens, "heads", axis=0, tiled=True),
        w_flat,
        preferred_element_type=jnp.float32,
    ).astype(jnp.bfloat16)
    slab_rows = projected.shape[0]
    projected = projected.reshape(slab_rows, 3, local_heads, HDIM)
    query = jnp.transpose(projected[:, 0], (1, 0, 2))
    keys = jnp.transpose(projected[:, 1], (1, 0, 2))
    values = jnp.transpose(projected[:, 2], (1, 0, 2))
    local_state = jnp.einsum("hsd,hse->hde", keys, values, preferred_element_type=jnp.float32)
    earlier_state = entering(
        local_state, "ctx", lambda first, second: first + second, jnp.zeros_like(local_state)
    )
    start_state = state_in + earlier_state
    tail = jnp.stack([keys, values], axis=0)
    arrived = from_behind(tail, "ctx", 1)
    past = jnp.transpose(past_kv.reshape(2, WINDOW, local_heads, HDIM), (0, 2, 1, 3))
    previous = jnp.where(lax.axis_index("ctx") == 0, past, arrived)
    all_keys = jnp.concatenate([previous[0], keys], axis=1)
    all_values = jnp.concatenate([previous[1], values], axis=1)
    block_rows = min(slab_rows, 512)
    block_count = slab_rows // block_rows
    scale = 1.0 / math.sqrt(HDIM)
    causal = jnp.arange(block_rows)[:, None] >= jnp.arange(block_rows)[None, :]
    offsets = jnp.arange(WINDOW + block_rows)[None, :] - jnp.arange(block_rows)[:, None]
    in_window = (offsets > 0) & (offsets <= WINDOW)

    def block_step(state, index):
        first = index * block_rows
        carried = jnp.einsum(
            "hsd,hde->hse", query.astype(jnp.float32), state, precision=lax.Precision.HIGHEST
        )
        inside = jnp.einsum("hsd,htd->hst", query, keys, preferred_element_type=jnp.float32)
        inside = jnp.where(causal[None], inside, 0.0).astype(jnp.bfloat16)
        linear = carried + jnp.einsum(
            "hst,hte->hse", inside, values, preferred_element_type=jnp.float32
        )
        scores = (
            jnp.einsum("hsd,htd->hst", query, all_keys, preferred_element_type=jnp.float32) * scale
        )
        scores = jnp.where(in_window[None], scores, -jnp.inf)
        top_score = jnp.max(scores, axis=-1, keepdims=True)
        expo = jnp.exp(scores - top_score)
        probs = (expo / jnp.sum(expo, axis=-1, keepdims=True)).astype(jnp.bfloat16)
        window_out = jnp.einsum(
            "hst,hte->hse", probs, all_values, preferred_element_type=jnp.float32
        )
        combined = (normalize(linear) + window_out).astype(jnp.bfloat16)
        new_state = state + jnp.einsum(
            "hsd,hse->hde", keys, values, preferred_element_type=jnp.float32
        )
        return (new_state, combined)

    _, outs = lax.scan(block_step, start_state, jnp.arange(block_count, dtype=jnp.int32))
    heads_out = jnp.transpose(outs, (0, 2, 1, 3)).reshape(slab_rows, inner_width)
    regrouped = lax.all_to_all(heads_out, "heads", split_axis=0, concat_axis=1, tiled=True)
    attn = jnp.dot(
        regrouped,
        lax.all_gather(w_out, "heads", axis=0, tiled=True),
        preferred_element_type=jnp.float32,
    )
    hidden_state = (tokens.astype(jnp.float32) + attn).astype(jnp.bfloat16)
    hidden_float = hidden_state.astype(jnp.float32)
    normed = normalize(hidden_float).astype(jnp.bfloat16)
    ctx_count = lax.axis_size("ctx")
    head_count = lax.axis_size("heads")
    exp_local = w_gate.shape[0]
    expert_count = exp_local * ctx_count * head_count
    top_count = expert_ids.shape[1]
    capacity = max(2, 2 * row_count * top_count // expert_count)
    devices = ctx_count * head_count
    if row_count * devices <= expert_count * capacity:
        return dense_experts(
            hidden_float, normed, w_gate, w_up, w_down, expert_ids, gate_weights, expert_count
        )
    picks = expert_ids.reshape(-1)
    onehot = (picks[:, None] == jnp.arange(expert_count, dtype=jnp.int32)[None, :]).astype(
        jnp.int32
    )
    earlier = jnp.cumsum(onehot, axis=0) - onehot
    slots = jnp.sum(onehot * earlier, axis=1)
    destination = picks * capacity + slots
    source_rows = jnp.arange(row_count * top_count, dtype=jnp.int32) // top_count
    outgoing = jnp.zeros((expert_count * capacity, model_width), jnp.bfloat16)
    outgoing = outgoing.at[destination].set(normed[source_rows])
    sendable = outgoing.reshape(expert_count, 1, capacity, model_width)
    arrived_rows = lax.all_to_all(
        sendable, ("ctx", "heads"), split_axis=0, concat_axis=1, tiled=True
    )
    e_count, n_count, c_count, d_count = arrived_rows.shape
    flat = arrived_rows.reshape(e_count, n_count * c_count, d_count)
    gate_act = jnp.einsum("erd,edf->erf", flat, w_gate, preferred_element_type=jnp.float32)
    up_act = jnp.einsum("erd,edf->erf", flat, w_up, preferred_element_type=jnp.float32)
    hid = (jax.nn.silu(gate_act) * up_act).astype(jnp.bfloat16)
    out_rows = jnp.einsum("erf,efd->erd", hid, w_down, preferred_element_type=jnp.float32)
    finished = out_rows.astype(jnp.bfloat16).reshape(e_count, n_count, c_count, d_count)
    returned = lax.all_to_all(finished, ("ctx", "heads"), split_axis=1, concat_axis=0, tiled=True)
    returned = returned.reshape(expert_count * capacity, model_width)
    picked = returned[destination].reshape(row_count, top_count, model_width).astype(jnp.float32)
    routed = jnp.sum(gate_weights[:, :, None] * picked, axis=1)
    return (hidden_float + routed).astype(jnp.bfloat16)


def solution(mesh):
    return jax.shard_map(
        on_device,
        mesh=mesh,
        in_specs=(
            P(("groups", "ctx", "heads"), None),
            P("heads", "groups", None),
            P(None, "groups", "heads"),
            P(None, None, "heads"),
            P("heads", None),
            P(("ctx", "heads"), None, None),
            P(("ctx", "heads"), None, None),
            P(("ctx", "heads"), None, None),
            P(("groups", "ctx", "heads"), None),
            P(("groups", "ctx", "heads"), None),
        ),
        out_specs=P(("groups", "ctx", "heads"), None),
        check_vma=False,
    )
```

profile of v0, /device:TPU:0, one launch (start us, length us, event | category | flops | bytes accessed | tf_op | source)
XLA Modules:
  0.0 328.5 jit_solution(8045174008604358506)
XLA Ops:
  8.0 2.6 copy.27
  10.6 46.7 %all-gather.5.cloned.1.call-done = bf16[512,2048]{1,0:T(8,128)(2,1)} async-done(((bf16[128,2048]{1,0:T(8,128)(2,1)}), bf16[512,2048]{1,0:T(8,128)(2,1)}) %all-gather.5.cloned.1.call-update) | async-done | bytes 2097168 | tf_op jit(solution)/shard_map/all_gather | solution.py:63
  57.3 3.1 convolution_convert_fusion
  61.3 5.4 %all-gather = bf16[512,128]{1,0:T(8,128)(2,1)S(1)} all-gather(bf16[128,128]{1,0:T(8,128)(2,1)S(1)} %convolution_convert_fusion.1), channel_id=2, replica_groups=mesh['groups'=2,'ctx'=4,'heads'=4] {'ctx'}, dimensions={0}, use_global_device_ids=true | all-gather | bytes 163840 | tf_op jit(solution)/shard_map/all_gather | solution.py:13
  66.7 1.0 copy.35
  67.8 1.7 copy.34
  69.4 1.6 pad_maximum_fusion
  71.1 3.0 collective-permute-start
  74.0 2.0 fusion.26
  76.0 2.3 multiply_reduce_fusion.1
  78.3 1.1 bitcast_select_fusion
  79.4 1.5 fusion.39
  82.1 0.8 copy.33
  82.8 3.5 %all-to-all-start = ((bf16[4,128,128]{1,2,0:T(8,128)(2,1)}), bf16[4,128,128]{1,2,0:T(8,128)(2,1)S(1)}, u32[]{:S(2)}, u32[]{:S(2)}) async-start(bf16[4,128,128]{1,2,0:T(8,128)(2,1)} %copy.33), calls=%async_computation | async-start | bytes 262144 | tf_op jit(solution)/shard_map/all_to_all | solution.py:118
  86.3 19.8 %all-gather.7.cloned.1.call-done = bf16[512,2048]{1,0:T(8,128)(2,1)} async-done(((bf16[128,2048]{1,0:T(8,128)(2,1)}), bf16[512,2048]{1,0:T(8,128)(2,1)}) %all-gather.7.cloned.1.call-update) | async-done | bytes 2097168 | tf_op jit(solution)/shard_map/all_gather | solution.py:121
  106.2 2.2 multiply_reduce_fusion
  108.4 1.0 copy-done.1
  109.4 0.9 multiply_convert_fusion.2
  110.5 33.1 %all_gather.22 = f32[2048,16]{0,1:T(8,128)S(1)} all-gather(f32[128,16]{0,1:T(8,128)S(1)} %select_reduce_fusion), channel_id=1, replica_groups=mesh['groups'=2,'ctx'=4,'heads'=4] {'ctx','heads'}, dimensions={0}, use_global_device_ids=true | all-gather | bytes 139264 | tf_op jit(solution)/shard_map/all_gather | solution.py:39
  143.6 41.7 %all-gather.9.cloned.1.call-done = bf16[2048,2048]{1,0:T(8,128)(2,1)} async-done(((bf16[128,2048]{1,0:T(8,128)(2,1)}), bf16[2048,2048]{1,0:T(8,128)(2,1)}) %all-gather.9.cloned.1.call-update) | async-done | bytes 8388624 | tf_op jit(solution)/shard_map/all_gather | solution.py:41
  185.3 11.7 %fusion.3 = f32[2048,768]{1,0:T(8,128)} fusion(bf16[2048,2048]{1,0:T(8,128)(2,1)} %all-gather.9.cloned.1.call-done, bf16[1,2048,768]{2,1,0:T(8,128)(2,1)} %param.17), kind=kOutput, calls=%fused_computation.5 | convolution fusion | flops 6442450944 | bytes 17825792 | tf_op jit(solution)/shard_map/dot_general | solution.py:44
  197.0 20.6 %multiply_convert_fusion = bf16[2048,2048]{1,0:T(8,128)(2,1)} fusion(f32[2048]{0:T(1024)S(1)} %bitcast.98, f32[2048,768]{1,0:T(8,128)} %fusion.3, bf16[2048,2048]{1,0:T(8,128)(2,1)} %all-gather.9.cloned.1.call-done, bf16[1,768,2048]{2,1,0:T(8,128)(2,1)S(1)} %copy-done, bf16[1,2048,768]{2,1,0:T(8,128)(2,1)} %param.18), kind=kOutput, calls=%fused_computation.1 | convolution fusion | flops 12902727680 | bytes 29368320 | tf_op jit(solution)/shard_map/dot_general | solution.py:47
  217.6 102.2 %reduce-scatter.2.cloned.1.call-done = bf16[128,2048]{1,0:T(8,128)(2,1)} async-done(((bf16[2048,2048]{1,0:T(8,128)(2,1)}), bf16[128,2048]{1,0:T(8,128)(2,1)}) %reduce-scatter.2.cloned.1.call-update) | async-done | bytes 524304 | tf_op jit(solution)/shard_map/reduce_scatter | solution.py:51
  319.7 2.3 add_convert_fusion
  (37 shorter events, 3.7 us)
Async XLA Ops:
  6.5 190.4 %copy-start = (bf16[1,768,2048]{2,1,0:T(8,128)(2,1)S(1)}, bf16[1,768,2048]{2,1,0:T(8,128)(2,1)}, u32[]{:S(2)}) copy-start(bf16[1,768,2048]{2,1,0:T(8,128)(2,1)} %param.19) | copy-start | bytes 9437188
  6.5 50.8 %all-gather.5.cloned.1.call-start = ((), (), s32[]{:S(2)}) async-start(), calls=%async_computation.2 | async-start | bytes 2621440 | tf_op jit(solution)/shard_map/all_gather | solution.py:63
  7.3 98.9 %all-gather.7.cloned.1.call-start = ((), (), s32[]{:S(2)}) async-start(), calls=%async_computation.3 | async-start | bytes 2621440 | tf_op jit(solution)/shard_map/all_gather | solution.py:121
  57.3 16.7 %copy-start.4 = (f32[1,128,128]{2,1,0:T(8,128)S(1)}, f32[1,128,128]{2,1,0:T(8,128)}, u32[]{:S(2)}) copy-start(f32[1,128,128]{2,1,0:T(8,128)} %param.13) | copy-start | bytes 196612
  60.4 6.3 %copy-start.3 = (bf16[512,384]{0,1:T(8,128)(2,1)}, bf16[512,384]{0,1:T(8,128)(2,1)S(1)}, u32[]{:S(2)}) copy-start(bf16[512,384]{0,1:T(8,128)(2,1)S(1)} %convolution_convert_fusion) | copy-start | bytes 1179652
  71.1 7.3 %collective-permute-start = (bf16[2,1,512,128]{3,2,1,0:T(8,128)(2,1)}, bf16[2,1,512,128]{3,2,1,0:T(8,128)(2,1)}, u32[]{:S(2)}, u32[]{:S(2)}) collective-permute-start(bf16[2,1,512,128]{3,2,1,0:T(8,128)(2,1)} %pad_maximum_fusion), channel_id=1, source_target_pairs={{0,4},{4,8},{8,12},{1,5},{5,9},{9,13},{2,6},{6,10},{10,14},{3,7},{... | collective-permute-start | bytes 786440 | tf_op jit(solution)/shard_map/ppermute | solution.py:25
  74.0 5.4 %copy-start.2 = (bf16[512,1,1,128]{3,0,2,1:T(8,128)(2,1)S(1)}, bf16[512,1,1,128]{3,0,2,1:T(8,128)(2,1)}, u32[]{:S(2)}) copy-start(bf16[512,1,1,128]{3,0,2,1:T(8,128)(2,1)} %copy.34) | copy-start | bytes 393220
  79.4 2.1 copy-start.7
  82.8 27.6 %copy-start.5 = (f32[128,8]{0,1:T(8,128)S(1)}, f32[128,8]{0,1:T(8,128)}, u32[]{:S(2)}) copy-start(f32[128,8]{0,1:T(8,128)} %param.21) | copy-start | bytes 12292
  82.8 27.6 %copy-start.6 = (s32[128,8]{0,1:T(8,128)S(1)}, s32[128,8]{0,1:T(8,128)}, u32[]{:S(2)}) copy-start(s32[128,8]{0,1:T(8,128)} %param.20) | copy-start | bytes 12292
  82.8 23.4 %all-to-all-start = ((bf16[4,128,128]{1,2,0:T(8,128)(2,1)}), bf16[4,128,128]{1,2,0:T(8,128)(2,1)S(1)}, u32[]{:S(2)}, u32[]{:S(2)}) async-start(bf16[4,128,128]{1,2,0:T(8,128)(2,1)} %copy.33), calls=%async_computation | async-start | bytes 262144 | tf_op jit(solution)/shard_map/all_to_all | solution.py:118
  86.3 99.0 %all-gather.9.cloned.1.call-start = ((), (), s32[]{:S(2)}) async-start(), calls=%async_computation.4 | async-start | bytes 8912896 | tf_op jit(solution)/shard_map/all_gather | solution.py:41
  108.4 1.0 copy-start.1
  110.4 209.4 %reduce-scatter.2.cloned.1.call-start = ((), (), s32[]{:S(2)}) async-start(), calls=%async_computation.5 | async-start | bytes 8912896 | tf_op jit(solution)/shard_map/reduce_scatter | solution.py:51
Sparse Core Ops, SparseCore 0:
  8.9 48.3 all-gather.4
  58.9 47.2 all-gather.6
  110.5 74.7 all-gather.8
  217.7 101.9 reduce-scatter.1
where the time goes:
time: 329 us
  waiting for transfers between devices  212 us (64%)
  matrix products  44.1 us (13%)
  blocking collectives  38.5 us (12%)
  between operations  13.3 us (4%)
  local copies, waits for them, and re-layouts  7.86 us (2%)
  starting transfers between devices  6.54 us (2%)
  other arithmetic  6.41 us (2%)
    reduce_scatter x1, waiting for transfers between devices, dense_experts(): lax.psum_scatter(total.astype(jnp.bfloat16), axes, scatter_dimension=0, t...  102 us
    all_gather x1, waiting for transfers between devices, on_device(): lax.all_gather(tokens, 'heads', axis=0, tiled=True)  46.7 us
    all_gather x1, waiting for transfers between devices, dense_experts(): rows = lax.all_gather(normed, axes, axis=0, tiled=True)  41.7 us
    all_gather x1, blocking collectives, dense_experts(): weights = lax.all_gather(table, axes, axis=0, tiled=True)  33.1 us
    dot_general x1, matrix products, dense_experts(): out_rows = jnp.dot(hid, w_down[e], preferred_element_type=jnp.float32)  20.6 us
    all_gather x1, waiting for transfers between devices, on_device(): lax.all_gather(w_out, 'heads', axis=0, tiled=True)  19.8 us
    dot_general x1, matrix products, dense_experts(): gate_act = jnp.dot(rows, w_gate[e], preferred_element_type=jnp.float32)  11.7 us
  transfers between devices with their start and end apart: 6, of which 4 were waited for; matrix products, arithmetic and copies ran while one was open for 6% of the time, Pallas kernels for 0%

commit v1 on v0

--- a/solution.py
+++ b/solution.py
@@ -1,3 +1,4 @@
+import functools
 import math
 import jax
 import jax.numpy as jnp
@@ -6,6 +7,31 @@
 
 HDIM = 128
 WINDOW = 512
+
+
+def replace_gates(unit, mesh_ax):
+    dev_n = lax.axis_size(mesh_ax)
+    formed = range(dev_n)
+    carry = map(lambda dev_i: (dev_i, (dev_i + 1) % dev_n), formed)
+    in_order = list(carry)
+    f_now = range(dev_n)
+    w_next = map(lambda dev_i: (dev_i, (dev_i - 1) % dev_n), f_now)
+    items = list(w_next)
+    local_part, item_now = ([unit], [unit])
+    for _ in range(dev_n // 2):
+        ready = lax.ppermute(local_part[-1], mesh_ax, in_order)
+        local_part.append(ready)
+    jj = 0
+    while jj < (dev_n - 1) // 2:
+        newest = lax.ppermute(item_now[-1], mesh_ax, items)
+        item_now.append(newest)
+        jj += 1
+    e_now = jnp.concatenate([*local_part[::-1], *item_now[1:]], axis=0)
+    b_next = lax.axis_index(mesh_ax)
+    return jnp.roll(e_now, (b_next - dev_n // 2) * unit.shape[0], axis=0)
+
+
+_handle_shifts_all = functools.partial(replace_gates, mesh_ax="heads")
 
 
 def entering(x, axis, join, neutral):
@@ -60,9 +86,7 @@
     local_heads = inner_width // HDIM
     w_flat = w_qkv.reshape(model_width, 3 * inner_width)
     projected = jnp.dot(
-        lax.all_gather(tokens, "heads", axis=0, tiled=True),
-        w_flat,
-        preferred_element_type=jnp.float32,
+        _handle_shifts_all(tokens), w_flat, preferred_element_type=jnp.float32
     ).astype(jnp.bfloat16)
     slab_rows = projected.shape[0]
     projected = projected.reshape(slab_rows, 3, local_heads, HDIM)

time: 329 us -> 331 us (level)
  waiting for transfers between devices: 212 us -> 196 us
  blocking collectives: 38.5 us -> 46.7 us
  local copies, waits for them, and re-layouts: 7.86 us -> 14.9 us
  starting transfers between devices: 6.54 us -> 9.9 us
    ppermute x0 -> x3, waiting for transfers between devices: none -> 51.8 us  [the longest x2 26.9 us: replace_gates(): ready = lax.ppermute(local_part[-1], mesh_ax, in_order)]
    all_gather x1 -> x0, waiting for transfers between devices: 46.7 us -> none  [on_device(): lax.all_gather(tokens, 'heads', axis=0, tiled=True)]
    all_gather x1, waiting for transfers between devices: 19.8 us -> 0.01 us  [on_device(): lax.all_gather(w_out, 'heads', axis=0, tiled=True)]
    all_to_all x0 -> x1, blocking collectives: none -> 8.93 us  [on_device(): lax.all_to_all(heads_out, 'heads', split_axis=0, concat_axis=1, tiled=True)]
    ppermute x0 -> x3, starting transfers between devices: none -> 6.88 us  [the longest x1 3.82 us: replace_gates(): newest = lax.ppermute(item_now[-1], mesh_ax, items)]
    unnamed x19 -> x28, local copies, waits for them, and re-layouts: 6.34 us -> 12.9 us
    all_to_all x1 -> x0, starting transfers between devices: 3.46 us -> none  [on_device(): lax.all_to_all(heads_out, 'heads', split_axis=0, concat_axis=1, tiled=True)]
  transfers between devices with their start and end apart: 6 -> 7, of which waited for: 4 -> 5; matrix products, arithmetic and copies ran while one was open for 6% -> 7% of each run, Pallas kernels for 0% -> 0%
where the time goes in v1:
time: 331 us; the launch traced here: 330 us
  waiting for transfers between devices  196 us (59%)
  blocking collectives  46.7 us (14%)
  matrix products  42 us (13%)
  local copies, waits for them, and re-layouts  14.9 us (5%)
  between operations  13.4 us (4%)
  starting transfers between devices  9.9 us (3%)
  other arithmetic  6.44 us (2%)
    reduce_scatter x1, waiting for transfers between devices, dense_experts(): lax.psum_scatter(total.astype(jnp.bfloat16), axes, scatter_dimension=0, t...  102 us
    all_gather x1, waiting for transfers between devices, dense_experts(): rows = lax.all_gather(normed, axes, axis=0, tiled=True)  42.4 us
    all_gather x1, blocking collectives, dense_experts(): weights = lax.all_gather(table, axes, axis=0, tiled=True)  32.4 us
    ppermute x2, waiting for transfers between devices, replace_gates(): ready = lax.ppermute(local_part[-1], mesh_ax, in_order)  26.9 us
    ppermute x1, waiting for transfers between devices, replace_gates(): newest = lax.ppermute(item_now[-1], mesh_ax, items)  24.9 us
    dot_general x1, matrix products, dense_experts(): out_rows = jnp.dot(hid, w_down[e], preferred_element_type=jnp.float32)  20.6 us
    unnamed x28, local copies, waits for them, and re-layouts  12.9 us
    dot_general x1, matrix products, dense_experts(): gate_act = jnp.dot(rows, w_gate[e], preferred_element_type=jnp.float32)  11.7 us
  transfers between devices with their start and end apart: 7, of which 5 were waited for; matrix products, arithmetic and copies ran while one was open for 7% of the time, Pallas kernels for 0%

profile of v1, /device:TPU:0, one launch (start us, length us, event | category | flops | bytes accessed | tf_op | source)
XLA Modules:
  0.0 329.8 jit_solution(11132390045069970315)
XLA Ops:
  6.5 3.1 collective-permute-start
  9.6 14.3 %collective-permute-done = bf16[128,2048]{1,0:T(8,128)(2,1)} collective-permute-done((bf16[128,2048]{1,0:T(8,128)(2,1)}, bf16[128,2048]{1,0:T(8,128)(2,1)}, u32[]{:S(2)}, u32[]{:S(2)}) %collective-permute-start) | collective-permute-done | bytes 524320 | tf_op jit(solution)/shard_map/ppermute | solution.py:22
  23.9 3.8 %collective-permute-start.2 = (bf16[128,2048]{1,0:T(8,128)(2,1)}, bf16[128,2048]{1,0:T(8,128)(2,1)}, u32[]{:S(2)}, u32[]{:S(2)}) collective-permute-start(bf16[128,2048]{1,0:T(8,128)(2,1)} %param.12), channel_id=1, source_target_pairs={{0,3},{1,0},{2,1},{3,2},{4,7},{5,4},{6,5},{7,6},{8,11},{9,8},{10,9... | collective-permute-start | bytes 1572872 | tf_op jit(solution)/shard_map/ppermute | solution.py:26
  27.8 2.7 copy.27
  30.5 12.6 %collective-permute-done.1 = bf16[128,2048]{1,0:T(8,128)(2,1)} collective-permute-done((bf16[128,2048]{1,0:T(8,128)(2,1)}, bf16[128,2048]{1,0:T(8,128)(2,1)}, u32[]{:S(2)}, u32[]{:S(2)}) %collective-permute-start.1) | collective-permute-done | bytes 524320 | tf_op jit(solution)/shard_map/ppermute | solution.py:22
  44.2 1.1 constant_dynamic-update-slice_fusion.6
  46.4 24.9 %collective-permute-done.2 = bf16[128,2048]{1,0:T(8,128)(2,1)} collective-permute-done((bf16[128,2048]{1,0:T(8,128)(2,1)}, bf16[128,2048]{1,0:T(8,128)(2,1)}, u32[]{:S(2)}, u32[]{:S(2)}) %collective-permute-start.2) | collective-permute-done | bytes 524320 | tf_op jit(solution)/shard_map/ppermute | solution.py:26
  72.3 1.1 constant_dynamic-update-slice_fusion.3
  77.6 5.4 %all-gather = bf16[512,128]{1,0:T(8,128)(2,1)S(1)} all-gather(bf16[128,128]{1,0:T(8,128)(2,1)S(1)} %convolution_convert_fusion), channel_id=2, replica_groups=mesh['groups'=2,'ctx'=4,'heads'=4] {'ctx'}, dimensions={0}, use_global_device_ids=true | all-gather | bytes 163840 | tf_op jit(solution)/shard_map/all_gather | solution.py:39
  84.1 1.7 copy.34
  85.7 1.6 pad_maximum_fusion
  87.3 2.9 collective-permute-start.3
  90.3 1.9 fusion.31
  92.2 2.3 multiply_reduce_fusion.1
  94.6 1.1 bitcast_select_fusion
  95.7 1.5 fusion.45
  98.5 8.9 %all_to_all.19 = bf16[4,128,128]{1,2,0:T(8,128)(2,1)S(1)} all-to-all(bf16[4,128,128]{1,2,0:T(8,128)(2,1)S(1)} %copy.33), channel_id=1, replica_groups=mesh['groups'=2,'ctx'=4,'heads'=4] {'heads'}, dimensions={0} | all-to-all | bytes 262144 | tf_op jit(solution)/shard_map/all_to_all | solution.py:142
  107.4 2.2 multiply_reduce_fusion
  111.7 32.4 %all_gather.18 = f32[2048,16]{0,1:T(8,128)S(1)} all-gather(f32[128,16]{0,1:T(8,128)S(1)} %select_reduce_fusion), channel_id=1, replica_groups=mesh['groups'=2,'ctx'=4,'heads'=4] {'ctx','heads'}, dimensions={0}, use_global_device_ids=true | all-gather | bytes 139264 | tf_op jit(solution)/shard_map/all_gather | solution.py:65
  144.1 42.4 %all-gather.6.cloned.1.call-done = bf16[2048,2048]{1,0:T(8,128)(2,1)} async-done(((bf16[128,2048]{1,0:T(8,128)(2,1)}), bf16[2048,2048]{1,0:T(8,128)(2,1)}) %all-gather.6.cloned.1.call-update) | async-done | bytes 8388624 | tf_op jit(solution)/shard_map/all_gather | solution.py:67
  186.5 11.7 %fusion.3 = f32[2048,768]{1,0:T(8,128)} fusion(bf16[2048,2048]{1,0:T(8,128)(2,1)} %all-gather.6.cloned.1.call-done, bf16[1,2048,768]{2,1,0:T(8,128)(2,1)} %param.17), kind=kOutput, calls=%fused_computation.5 | convolution fusion | flops 6442450944 | bytes 17825792 | tf_op jit(solution)/shard_map/dot_general | solution.py:70
  198.2 20.6 %multiply_convert_fusion = bf16[2048,2048]{1,0:T(8,128)(2,1)} fusion(f32[2048]{0:T(1024)S(1)} %bitcast.97, f32[2048,768]{1,0:T(8,128)} %fusion.3, bf16[2048,2048]{1,0:T(8,128)(2,1)} %all-gather.6.cloned.1.call-done, bf16[1,768,2048]{2,1,0:T(8,128)(2,1)S(1)} %copy-done, bf16[1,2048,768]{2,1,0:T(8,128)(2,1)} %param.18), kind=kOutput, calls=%fused_computation.1 | convolution fusion | flops 12902727680 | bytes 29368320 | tf_op jit(solution)/shard_map/dot_general | solution.py:73
  218.8 102.2 %reduce-scatter.2.cloned.1.call-done = bf16[128,2048]{1,0:T(8,128)(2,1)} async-done(((bf16[2048,2048]{1,0:T(8,128)(2,1)}), bf16[128,2048]{1,0:T(8,128)(2,1)}) %reduce-scatter.2.cloned.1.call-update) | async-done | bytes 524304 | tf_op jit(solution)/shard_map/reduce_scatter | solution.py:77
  321.0 2.3 add_convert_fusion
  (49 shorter events, 11.7 us)
Async XLA Ops:
  6.5 191.7 %copy-start = (bf16[1,768,2048]{2,1,0:T(8,128)(2,1)S(1)}, bf16[1,768,2048]{2,1,0:T(8,128)(2,1)}, u32[]{:S(2)}) copy-start(bf16[1,768,2048]{2,1,0:T(8,128)(2,1)} %param.19) | copy-start | bytes 9437188
  6.5 100.9 %all-gather.4.cloned.1.call-start = ((), (), s32[]{:S(2)}) async-start(), calls=%async_computation.2 | async-start | bytes 2621440 | tf_op jit(solution)/shard_map/all_gather | solution.py:145
  6.5 17.3 %collective-permute-start = (bf16[128,2048]{1,0:T(8,128)(2,1)}, bf16[128,2048]{1,0:T(8,128)(2,1)}, u32[]{:S(2)}, u32[]{:S(2)}) collective-permute-start(bf16[128,2048]{1,0:T(8,128)(2,1)} %param.12), channel_id=1, source_target_pairs={{0,1},{1,2},{2,3},{3,0},{4,5},{5,6},{6,7},{7,4},{8,9},{9,10},{10,1... | collective-permute-start | bytes 1572872 | tf_op jit(solution)/shard_map/ppermute | solution.py:22
  23.9 19.2 %collective-permute-start.1 = (bf16[128,2048]{1,0:T(8,128)(2,1)}, bf16[128,2048]{1,0:T(8,128)(2,1)}, u32[]{:S(2)}, u32[]{:S(2)}) collective-permute-start(bf16[128,2048]{1,0:T(8,128)(2,1)} %collective-permute-done), channel_id=1, source_target_pairs={{0,1},{1,2},{2,3},{3,0},{4,5},{5,6},{6,7},{7,4},{8,9},{9,10},{10,1... | collective-permute-start | bytes 1572872 | tf_op jit(solution)/shard_map/ppermute | solution.py:22
  23.9 47.4 %collective-permute-start.2 = (bf16[128,2048]{1,0:T(8,128)(2,1)}, bf16[128,2048]{1,0:T(8,128)(2,1)}, u32[]{:S(2)}, u32[]{:S(2)}) collective-permute-start(bf16[128,2048]{1,0:T(8,128)(2,1)} %param.12), channel_id=1, source_target_pairs={{0,3},{1,0},{2,1},{3,2},{4,7},{5,4},{6,5},{7,6},{8,11},{9,8},{10,9... | collective-permute-start | bytes 1572872 | tf_op jit(solution)/shard_map/ppermute | solution.py:26
  27.7 158.8 %all-gather.6.cloned.1.call-start = ((), (), s32[]{:S(2)}) async-start(), calls=%async_computation.3 | async-start | bytes 8912896 | tf_op jit(solution)/shard_map/all_gather | solution.py:67
  30.4 44.1 %copy-start.2 = (bf16[128,2048]{1,0:T(8,128)(2,1)S(1)}, bf16[128,2048]{1,0:T(8,128)(2,1)}, u32[]{:S(2)}) copy-start(bf16[128,2048]{1,0:T(8,128)(2,1)} %param.12) | copy-start | bytes 1572868
  30.4 45.2 %copy-start.3 = (bf16[2048,3,128]{0,2,1:T(8,128)(2,1)S(1)}, bf16[2048,3,128]{0,2,1:T(8,128)(2,1)}, u32[]{:S(2)}) copy-start(bf16[2048,3,128]{0,2,1:T(8,128)(2,1)} %copy.27) | copy-start | bytes 4718596
  75.7 14.6 %copy-start.5 = (f32[1,128,128]{2,1,0:T(8,128)S(1)}, f32[1,128,128]{2,1,0:T(8,128)}, u32[]{:S(2)}) copy-start(f32[1,128,128]{2,1,0:T(8,128)} %param.13) | copy-start | bytes 196612
  76.7 6.3 %copy-start.4 = (bf16[512,384]{0,1:T(8,128)(2,1)}, bf16[512,384]{0,1:T(8,128)(2,1)S(1)}, u32[]{:S(2)}) copy-start(bf16[512,384]{0,1:T(8,128)(2,1)S(1)} %fusion.15) | copy-start | bytes 1179652
  87.3 7.2 %collective-permute-start.3 = (bf16[2,1,512,128]{3,2,1,0:T(8,128)(2,1)}, bf16[2,1,512,128]{3,2,1,0:T(8,128)(2,1)}, u32[]{:S(2)}, u32[]{:S(2)}) collective-permute-start(bf16[2,1,512,128]{3,2,1,0:T(8,128)(2,1)} %pad_maximum_fusion), channel_id=1, source_target_pairs={{0,4},{4,8},{8,12},{1,5},{5,9},{9,13},{2,6},{6,10},{10,14},{3,7},{... | collective-permute-start | bytes 786440 | tf_op jit(solution)/shard_map/ppermute | solution.py:51
  94.5 3.2 copy-start.8
  98.3 13.3 %copy-start.6 = (f32[128,8]{0,1:T(8,128)S(1)}, f32[128,8]{0,1:T(8,128)}, u32[]{:S(2)}) copy-start(f32[128,8]{0,1:T(8,128)} %param.21) | copy-start | bytes 12292
  98.3 13.3 %copy-start.7 = (s32[128,8]{0,1:T(8,128)S(1)}, s32[128,8]{0,1:T(8,128)}, u32[]{:S(2)}) copy-start(s32[128,8]{0,1:T(8,128)} %param.20) | copy-start | bytes 12292
  109.6 1.0 copy-start.1
  111.6 209.4 %reduce-scatter.2.cloned.1.call-start = ((), (), s32[]{:S(2)}) async-start(), calls=%async_computation.4 | async-start | bytes 8912896 | tf_op jit(solution)/shard_map/reduce_scatter | solution.py:77
Sparse Core Ops, SparseCore 0:
  27.8 54.5 all-gather.3
  111.7 74.7 all-gather.5
  218.9 102.0 reduce-scatter.1
